TPU v7x, 32 devices: a whole 2x2x4 slice. The times are simulated.
32 devices in a mesh: wrow: 16 (over z, y, x), kblk: 2 (over core).
Axes of the slice: x: 2, y: 2, z: 4, core: 2. Of those that a mesh axis runs over, the one named last changes fastest.
Arguments:
- conduction: bfloat16 [2, 4, 64, 16384], P('kblk', None, None, 'wrow'), may hold values from -6 to 6
- valence: bfloat16 [2, 4, 64, 16384], P(None, None, 'wrow', 'kblk'), may hold values from -6 to 6
- screened: bfloat16 [4, 16384, 16384], P(None, 'wrow', 'kblk'), may hold values from -0.00036621094 to 0.00036621094
- pair_block: int32 [2, 4], replicated, may hold values from 0 to 3, as said below
Outputs:
- kernel: float32 [2, 64, 256], P('kblk', 'wrow')
Inputs may be any that keep to these rules, and one draw needn't show every extreme that they name: `pair_block`: every one of the 4 blocks is selected by at least one pair and by at most 3 pairs; one block by exactly 3 pairs.
All inputs are finite; a program needn't handle non-finite values.
Results may differ from a plain program's by a relative error of at most 0.0029.
Values may be sent and summed in bfloat16 or wider, within the bound.
No kernel may reach another device: no remote copies, remote signals or barrier semaphores. Data moves between devices by JAX's collectives and lax.ppermute only.
A program may use at most 128 MiB of HBM per device.

v0:
```python
import jax
import jax.numpy as jnp
from jax import lax
from jax.sharding import PartitionSpec as P

C = 8
V = 8


def per_device(conduction, valence, screened, pair_block):
    gathered_cond = lax.all_gather(conduction, "kblk", axis=0, tiled=True)
    gathered_vale = lax.all_gather(valence, "wrow", axis=2, tiled=True)
    k_count = gathered_cond.shape[0]
    kp_count = gathered_cond.shape[1]
    pair_count = k_count * kp_count
    row_width = gathered_cond.shape[3]
    col_width = gathered_vale.shape[3]
    cond_flat = gathered_cond.reshape(pair_count, C * C, row_width)
    vale_flat = gathered_vale.reshape(pair_count, V * V, col_width)
    flat_blocks = pair_block.reshape(pair_count)
    pair_ids = jnp.arange(pair_count, dtype=jnp.int32)
    capacity = 3 * pair_count // 8
    block_count = screened.shape[0]

    def one_block(block, total):
        sort_keys = jnp.where(flat_blocks == block, 0, pair_count) + pair_ids
        chosen = jnp.argsort(sort_keys)[:capacity]
        present = (flat_blocks[chosen] == block).astype(jnp.float32)
        vale_sel = jnp.take(vale_flat, chosen, axis=0)
        cond_sel = jnp.take(cond_flat, chosen, axis=0)
        w_tile = lax.dynamic_index_in_dim(screened, block, 0, keepdims=False)
        screened_vale = jnp.einsum(
            "pvh,gh->pvg", vale_sel, w_tile, preferred_element_type=jnp.float32
        ).astype(jnp.bfloat16)
        tiles = jnp.einsum(
            "pcg,pvg->pcv", cond_sel, screened_vale, preferred_element_type=jnp.float32
        )
        placer = (pair_ids[:, None] == chosen[None, :]).astype(jnp.float32) * present[None, :]
        return total + jnp.einsum("sp,pcv->scv", placer, tiles, precision=lax.Precision.HIGHEST)

    terms = lax.fori_loop(
        0, block_count, one_block, jnp.zeros((pair_count, C * C, V * V), jnp.float32)
    )
    terms = terms.reshape(k_count, kp_count, C, C, V, V).transpose(0, 2, 4, 1, 3, 5)
    terms = terms.reshape(k_count, C * V, kp_count * C * V)
    by_block = lax.psum_scatter(terms, "kblk", scatter_dimension=0, tiled=True)
    return lax.psum_scatter(by_block, "wrow", scatter_dimension=1, tiled=True)


def solution(mesh):
    return jax.shard_map(
        per_device,
        mesh=mesh,
        in_specs=(
            P("kblk", None, None, "wrow"),
            P(None, None, "wrow", "kblk"),
            P(None, "wrow", "kblk"),
            P(),
        ),
        out_specs=P("kblk", "wrow", None),
        check_vma=False,
    )
```

profile of v0, /device:TPU:0, one launch (start us, length us, event | category | flops | bytes accessed | tf_op | source)
XLA Modules:
  0.0 346.6 jit_solution(13563379429917125649)
XLA Ops:
  6.5 2.2 copy.8
  10.4 114.8 %all-gather.5.cloned.1.call-done = bf16[2,4,64,8192]{3,1,0,2:T(4,128)(2,1)} async-done(((bf16[2,4,4,8192]{3,1,0,2:T(4,128)(2,1)}), bf16[2,4,64,8192]{3,1,0,2:T(4,128)(2,1)}) %all-gather.5.cloned.1.call-update) | async-done | bytes 8388624 | tf_op jit(solution)/shard_map/all_gather | solution.py:12
  125.2 11.2 %copy.11 = bf16[2,4,64,8192]{3,2,1,0:T(8,128)(2,1)} copy(bf16[2,4,64,8192]{3,1,0,2:T(4,128)(2,1)} %all-gather.5.cloned.1.call-done) | data formatting | bytes 16777216
  136.3 78.8 %while.15 = (s32[]{:T(128)}, f32[8,64,64]{2,0,1:T(8,128)S(1)}, s32[8]{0:T(128)S(1)}, bf16[8,64,1024]{2,1,0:T(8,128)(2,1)}, bf16[8,64,8192]{2,1,0:T(8,128)(2,1)},...) while((s32[]{:T(128)}, f32[8,64,64]{2,0,1:T(8,128)S(1)}, s32[8]{0:T(128)S(1)}, ...), condition=%wide.region_2.3_spmd.clone.clone, body=%wide.region_0.2_spmd.clone.clone.sunk | while | flops 3249603584 | bytes 28546016 | solution.py:41
  137.3 4.1 %gather_fusion = bf16[3,64,8192]{2,1,0:T(8,128)(2,1)S(1)} fusion(bf16[8,64,8192]{2,1,0:T(8,128)(2,1)} %get-tuple-element.260, s32[1024]{0:T(1024)S(1)} %pad_clamp_fusion.2), kind=kCustom, calls=%fused_computation.2.clone.clone.1 | custom fusion | bytes 6291468 | tf_op jit(solution)/shard_map/while/body/eval_jaxpr/jit(_take)/gather | solution.py:29
  141.5 10.3 %fusion.45 = bf16[3,64,1024]{2,1,0:T(8,128)(2,1)} fusion(bf16[4,1024,8192]{2,1,0:T(8,128)(2,1)} %get-tuple-element.261, s32[]{:T(128)} %get-tuple-element.248, bf16[3,64,8192]{2,1,0:T(8,128)(2,1)S(1)} %gather_fusion, pred[3]{0:T(512)(128)(4,1)S(1)} %get-tuple-element.239), kind=kOutput, calls=%fused_computation.10.clone.1 | convolution fusion | flops 3222994944 | bytes 20316676 | tf_op jit(solution)/shard_map/while/body/eval_jaxpr/pvh,gh->pvg/dot_general | solution.py:32
  151.8 1.8 gather_fusion.1
  153.6 1.3 fusion.46
  157.1 4.1 %gather_fusion = bf16[3,64,8192]{2,1,0:T(8,128)(2,1)S(1)} fusion(bf16[8,64,8192]{2,1,0:T(8,128)(2,1)} %get-tuple-element.260, s32[1024]{0:T(1024)S(1)} %pad_clamp_fusion.2), kind=kCustom, calls=%fused_computation.2.clone.clone.1 | custom fusion | bytes 6291468 | tf_op jit(solution)/shard_map/while/body/eval_jaxpr/jit(_take)/gather | solution.py:29
  161.2 10.3 %fusion.45 = bf16[3,64,1024]{2,1,0:T(8,128)(2,1)} fusion(bf16[4,1024,8192]{2,1,0:T(8,128)(2,1)} %get-tuple-element.261, s32[]{:T(128)} %get-tuple-element.248, bf16[3,64,8192]{2,1,0:T(8,128)(2,1)S(1)} %gather_fusion, pred[3]{0:T(512)(128)(4,1)S(1)} %get-tuple-element.239), kind=kOutput, calls=%fused_computation.10.clone.1 | convolution fusion | flops 3222994944 | bytes 20316676 | tf_op jit(solution)/shard_map/while/body/eval_jaxpr/pvh,gh->pvg/dot_general | solution.py:32
  171.5 1.8 gather_fusion.1
  173.3 1.3 fusion.46
  176.8 4.1 %gather_fusion = bf16[3,64,8192]{2,1,0:T(8,128)(2,1)S(1)} fusion(bf16[8,64,8192]{2,1,0:T(8,128)(2,1)} %get-tuple-element.260, s32[1024]{0:T(1024)S(1)} %pad_clamp_fusion.2), kind=kCustom, calls=%fused_computation.2.clone.clone.1 | custom fusion | bytes 6291468 | tf_op jit(solution)/shard_map/while/body/eval_jaxpr/jit(_take)/gather | solution.py:29
  180.9 10.3 %fusion.45 = bf16[3,64,1024]{2,1,0:T(8,128)(2,1)} fusion(bf16[4,1024,8192]{2,1,0:T(8,128)(2,1)} %get-tuple-element.261, s32[]{:T(128)} %get-tuple-element.248, bf16[3,64,8192]{2,1,0:T(8,128)(2,1)S(1)} %gather_fusion, pred[3]{0:T(512)(128)(4,1)S(1)} %get-tuple-element.239), kind=kOutput, calls=%fused_computation.10.clone.1 | convolution fusion | flops 3222994944 | bytes 20316676 | tf_op jit(solution)/shard_map/while/body/eval_jaxpr/pvh,gh->pvg/dot_general | solution.py:32
  191.2 1.8 gather_fusion.1
  193.0 1.3 fusion.46
  196.5 4.1 %gather_fusion = bf16[3,64,8192]{2,1,0:T(8,128)(2,1)S(1)} fusion(bf16[8,64,8192]{2,1,0:T(8,128)(2,1)} %get-tuple-element.260, s32[1024]{0:T(1024)S(1)} %pad_clamp_fusion.2), kind=kCustom, calls=%fused_computation.2.clone.clone.1 | custom fusion | bytes 6291468 | tf_op jit(solution)/shard_map/while/body/eval_jaxpr/jit(_take)/gather | solution.py:29
  200.6 10.3 %fusion.45 = bf16[3,64,1024]{2,1,0:T(8,128)(2,1)} fusion(bf16[4,1024,8192]{2,1,0:T(8,128)(2,1)} %get-tuple-element.261, s32[]{:T(128)} %get-tuple-element.248, bf16[3,64,8192]{2,1,0:T(8,128)(2,1)S(1)} %gather_fusion, pred[3]{0:T(512)(128)(4,1)S(1)} %get-tuple-element.239), kind=kOutput, calls=%fused_computation.10.clone.1 | convolution fusion | flops 3222994944 | bytes 20316676 | tf_op jit(solution)/shard_map/while/body/eval_jaxpr/pvh,gh->pvg/dot_general | solution.py:32
  210.9 1.8 gather_fusion.1
  212.7 1.3 fusion.46
  215.8 3.0 copy.17
  218.8 3.5 reshape.32
  222.3 6.4 %reduce-scatter.3.cloned.1.call-done = f32[1,64,256]{2,1,0:T(8,128)} async-done(((f32[2,64,256]{2,1,0:T(8,128)}), f32[1,64,256]{2,1,0:T(8,128)}) %reduce-scatter.3.cloned.1.call-update) | async-done | bytes 65552 | tf_op jit(solution)/shard_map/reduce_scatter | solution.py:46
  230.0 108.7 %all-reduce.3.cloned.1.call-done = f32[1,64,256]{2,1,0:T(8,128)} async-done(((f32[1,64,256]{2,1,0:T(8,128)}), f32[1,64,256]{2,1,0:T(8,128)}) %all-reduce.3.cloned.1.call-update) | async-done | bytes 65552
  (48 shorter events, 12.7 us)
Async XLA Ops:
  6.5 118.6 %all-gather.5.cloned.1.call-start = ((), (), s32[]{:S(2)}) async-start(), calls=%async_computation.2 | async-start | bytes 8912896 | tf_op jit(solution)/shard_map/all_gather | solution.py:12
  8.8 127.6 %all-gather.3.cloned.1.call-start = ((), (), s32[]{:S(2)}) async-start(), calls=%async_computation.1 | async-start | bytes 1572864 | tf_op jit(solution)/shard_map/all_gather | solution.py:11
  9.5 219.2 %reduce-scatter.3.cloned.1.call-start = ((), (), s32[]{:S(2)}) async-start(), calls=%async_computation.3 | async-start | bytes 196608 | tf_op jit(solution)/shard_map/reduce_scatter | solution.py:46
  215.8 13.0 %copy-start = (u32[32]{0:T(128)S(1)}, u32[32]{0:T(128)}, u32[]{:S(2)}) copy-start(u32[32]{0:T(128)} %constant.81) | copy-start | bytes 388
  222.2 116.5 %all-reduce.3.cloned.1.call-start = ((), (), s32[]{:S(2)}) async-start(), calls=%async_computation.4 | async-start | bytes 131072
Sparse Core Ops, SparseCore 0:
  10.1 115.0 all-gather.4
  126.7 7.1 all-gather.2
  222.4 6.3 reduce-scatter.2
  234.1 104.6 all-reduce.2
where the time goes:
time: 347 us
  waiting for transfers between devices  231 us (67%)
  local copies, waits for them, and re-layouts  49.3 us (14%)
  matrix products  48.4 us (14%)
  between operations  13.8 us (4%)
  other arithmetic  3.96 us (1%)
    all_gather x1, waiting for transfers between devices, per_device(): gathered_vale = lax.all_gather(valence, 'wrow', axis=2, tiled=True)  115 us
    unnamed x5, waiting for transfers between devices  109 us
    dot_general x4, matrix products, one_block(): jnp.einsum('pvh,gh->pvg', vale_sel, w_tile, preferred_element_type=jnp.fl...  41.1 us
    gather x4, local copies, waits for them, and re-layouts, one_block(): vale_sel = jnp.take(vale_flat, chosen, axis=0)  16.5 us
    unnamed x6, local copies, waits for them, and re-layouts  15.3 us
    gather x4, local copies, waits for them, and re-layouts, one_block(): cond_sel = jnp.take(cond_flat, chosen, axis=0)  7.18 us
  transfers between devices with their start and end apart: 4, of which 3 were waited for; matrix products, arithmetic and copies ran while one was open for 4% of the time, Pallas kernels for 0%

commit v1 on v0

--- a/solution.py
+++ b/solution.py
@@ -9,7 +9,23 @@
 
 def per_device(conduction, valence, screened, pair_block):
     gathered_cond = lax.all_gather(conduction, "kblk", axis=0, tiled=True)
-    gathered_vale = lax.all_gather(valence, "wrow", axis=2, tiled=True)
+
+    def connect_the_space(xs, group_axis):
+        p_next, t_next, all_values = (
+            lax.psum(1, group_axis),
+            lax.axis_index(group_axis),
+            xs.shape[2],
+        )
+        answer, frame_out = (xs, 1)
+        while frame_out < p_next:
+            trail = []
+            for at in range(p_next):
+                trail.append((at, (at - frame_out) % p_next))
+            answer = jnp.concatenate([answer, lax.ppermute(answer, group_axis, trail)], 2)
+            frame_out = 2 * frame_out
+        return jnp.roll(answer, t_next * all_values, 2)
+
+    gathered_vale = connect_the_space(valence, "wrow")
     k_count = gathered_cond.shape[0]
     kp_count = gathered_cond.shape[1]
     pair_count = k_count * kp_count

time: 347 us -> 572 us (1.65)
  waiting for transfers between devices: 231 us -> 381 us
  local copies, waits for them, and re-layouts: 49.3 us -> 107 us
  starting transfers between devices: 0.12 us -> 9.1 us
  other arithmetic: 3.96 us -> 10.1 us
    ppermute x0 -> x4, waiting for transfers between devices: none -> 260 us  [connect_the_space(): lax.ppermute(answer, group_axis, trail)]
    all_gather x1 -> x0, waiting for transfers between devices: 115 us -> none  [per_device(): gathered_vale = lax.all_gather(valence, 'wrow', axis=2, tiled=True)]
    concatenate x0 -> x1, local copies, waits for them, and re-layouts: none -> 62.4 us  [connect_the_space(): return jnp.roll(answer, t_next * all_values, 2)]
    unnamed x6 -> x10, local copies, waits for them, and re-layouts: 15.3 us -> 1.9 us
    ppermute x0 -> x4, starting transfers between devices: none -> 9.01 us  [connect_the_space(): lax.ppermute(answer, group_axis, trail)]
    dynamic_slice x0 -> x1, local copies, waits for them, and re-layouts: none -> 8.96 us  [connect_the_space(): return jnp.roll(answer, t_next * all_values, 2)]
    reduce_scatter x1, waiting for transfers between devices: 6.44 us -> 12.8 us  [per_device(): by_block = lax.psum_scatter(terms, 'kblk', scatter_dimension=0, tiled=True)]
    concatenate x0 -> x3, other arithmetic: none -> 6.22 us  [connect_the_space(): jnp.concatenate([answer, lax.ppermute(answer, group_axis, trail)], 2)]
  transfers between devices with their start and end apart: 4 -> 7, of which waited for: 3 -> 6; matrix products, arithmetic and copies ran while one was open for 4% -> 13% of each run, Pallas kernels for 0% -> 0%
where the time goes in v1:
time: 572 us; the launch traced here: 569 us
  waiting for transfers between devices  381 us (67%)
  local copies, waits for them, and re-layouts  107 us (19%)
  matrix products  48.2 us (8%)
  between operations  13.9 us (2%)
  other arithmetic  10.1 us (2%)
  starting transfers between devices  9.1 us (2%)
    ppermute x4, waiting for transfers between devices, connect_the_space(): lax.ppermute(answer, group_axis, trail)  260 us
    unnamed x4, waiting for transfers between devices  109 us
    concatenate x1, local copies, waits for them, and re-layouts, connect_the_space(): return jnp.roll(answer, t_next * all_values, 2)  62.4 us
    dot_general x4, matrix products, one_block(): jnp.einsum('pvh,gh->pvg', vale_sel, w_tile, preferred_element_type=jnp.fl...  40.9 us
    gather x4, local copies, waits for them, and re-layouts, one_block(): vale_sel = jnp.take(vale_flat, chosen, axis=0)  16.5 us
    reduce_scatter x1, waiting for transfers between devices, per_device(): by_block = lax.psum_scatter(terms, 'kblk', scatter_dimension=0, tiled=True)  12.8 us
  transfers between devices with their start and end apart: 7, of which 6 were waited for; matrix products, arithmetic and copies ran while one was open for 13% of the time, Pallas kernels for 0%

profile of v1, /device:TPU:0, one launch (start us, length us, event | category | flops | bytes accessed | tf_op | source)
XLA Modules:
  0.0 569.3 jit_solution(16578556280611589363)
XLA Ops:
  6.5 7.0 %collective-permute-start = (bf16[2,4,4,8192]{3,2,1,0:T(4,128)(2,1)}, bf16[2,4,4,8192]{3,2,1,0:T(4,128)(2,1)S(1)}, u32[]{:S(2)}, u32[]{:S(2)}) collective-permute-start(bf16[2,4,4,8192]{3,2,1,0:T(4,128)(2,1)} %param.7), channel_id=1, source_target_pairs={{0,30},{2,0},{4,2},{6,4},{8,6},{10,8},{12,10},{14,12},{16,14},{18,... | collective-permute-start | bytes 1572872 | tf_op jit(solution)/shard_map/ppermute | solution.py:24
  13.5 11.5 %collective-permute-done = bf16[2,4,4,8192]{3,2,1,0:T(4,128)(2,1)S(1)} collective-permute-done((bf16[2,4,4,8192]{3,2,1,0:T(4,128)(2,1)}, bf16[2,4,4,8192]{3,2,1,0:T(4,128)(2,1)S(1)}, u32[]{:S(2)}, u32[]{:S(2)}) %collective-permute-start) | collective-permute-done | bytes 524320 | tf_op jit(solution)/shard_map/ppermute | solution.py:24
  28.2 22.6 %collective-permute-done.1 = bf16[2,4,8,8192]{3,2,1,0:T(8,128)(2,1)S(1)} collective-permute-done((bf16[2,4,8,8192]{3,2,1,0:T(8,128)(2,1)S(1)}, bf16[2,4,8,8192]{3,2,1,0:T(8,128)(2,1)S(1)}, u32[]{:S(2)}, u32[]{:S(2)}) %collective-permute-start.1) | collective-permute-done | bytes 1048608 | tf_op jit(solution)/shard_map/ppermute | solution.py:24
  50.8 1.9 pad_maximum_fusion.1
  53.3 45.2 %collective-permute-done.2 = bf16[2,4,16,8192]{3,2,1,0:T(8,128)(2,1)S(1)} collective-permute-done((bf16[2,4,16,8192]{3,2,1,0:T(8,128)(2,1)S(1)}, bf16[2,4,16,8192]{3,2,1,0:T(8,128)(2,1)S(1)}, u32[]{:S(2)}, u32[]{:S(2)}) %collective-permute-start.2) | collective-permute-done | bytes 2097184 | tf_op jit(solution)/shard_map/ppermute | solution.py:24
  98.5 2.6 pad_maximum_fusion
  101.3 180.3 %collective-permute-done.3 = bf16[2,4,32,8192]{3,2,1,0:T(8,128)(2,1)} collective-permute-done((bf16[2,4,32,8192]{3,2,1,0:T(8,128)(2,1)}, bf16[2,4,32,8192]{3,2,1,0:T(8,128)(2,1)}, u32[]{:S(2)}, u32[]{:S(2)}) %collective-permute-start.3) | collective-permute-done | bytes 4194336 | tf_op jit(solution)/shard_map/ppermute | solution.py:24
  281.6 62.4 %concatenate.21 = bf16[2,4,128,8192]{3,2,1,0:T(8,128)(2,1)} concatenate(bf16[2,4,4,8192]{3,2,1,0:T(4,128)(2,1)} %param.7, bf16[2,4,4,8192]{3,2,1,0:T(4,128)(2,1)} %copy-done.1, bf16[2,4,8,8192]{3,2,1,0:T(8,128)(2,1)S(1)} %collective-permute-done.1, bf16[2,4,16,8192]{3,2,1,0:T(8,128)(2,1)S(1)} %collective-permute-done.2, bf16[2,4,32,8192]{3,2,1,0:T(8,128)(2,1)} %collective-permute-done.3, ...), dimensions={2} | concatenate | bytes 33554432 | tf_op jit(solution)/shard_map/jit(_roll_dynamic)/concatenate | solution.py:26
  343.9 9.0 %constant_dynamic-slice_fusion.1 = bf16[2,4,64,8192]{3,2,1,0:T(8,128)(2,1)} fusion(bf16[2,4,128,8192]{3,2,1,0:T(8,128)(2,1)} %concatenate.21, s32[]{:T(128)S(6)} %select_n.56), kind=kLoop, calls=%fused_computation.38 | loop fusion | bytes 16777220 | tf_op jit(solution)/shard_map/jit(_roll_dynamic)/dynamic_slice | solution.py:26
  352.9 78.6 %while.15 = (s32[]{:T(128)}, f32[8,64,64]{2,0,1:T(8,128)S(1)}, s32[8]{0:T(128)S(1)}, bf16[8,64,1024]{2,1,0:T(8,128)(2,1)}, bf16[8,64,8192]{2,1,0:T(8,128)(2,1)},...) while((s32[]{:T(128)}, f32[8,64,64]{2,0,1:T(8,128)S(1)}, s32[8]{0:T(128)S(1)}, ...), condition=%wide.region_2.3_spmd.clone.clone, body=%wide.region_0.2_spmd.clone.clone.sunk | while | flops 3249603584 | bytes 28546016 | solution.py:57
  353.9 4.1 gather_fusion
  358.0 10.2 %fusion.45 = bf16[3,64,1024]{2,1,0:T(8,128)(2,1)} fusion(bf16[4,1024,8192]{2,1,0:T(8,128)(2,1)} %get-tuple-element.255, s32[]{:T(128)} %get-tuple-element.242, bf16[3,64,8192]{2,1,0:T(8,128)(2,1)S(1)} %gather_fusion, pred[3]{0:T(512)(128)(4,1)S(1)} %get-tuple-element.233), kind=kOutput, calls=%fused_computation.10.clone.1 | convolution fusion | flops 3222994944 | bytes 20316676 | tf_op jit(solution)/shard_map/while/body/eval_jaxpr/pvh,gh->pvg/dot_general | solution.py:48
  368.2 1.8 gather_fusion.1
  373.5 4.1 gather_fusion
  377.7 10.2 %fusion.45 = bf16[3,64,1024]{2,1,0:T(8,128)(2,1)} fusion(bf16[4,1024,8192]{2,1,0:T(8,128)(2,1)} %get-tuple-element.255, s32[]{:T(128)} %get-tuple-element.242, bf16[3,64,8192]{2,1,0:T(8,128)(2,1)S(1)} %gather_fusion, pred[3]{0:T(512)(128)(4,1)S(1)} %get-tuple-element.233), kind=kOutput, calls=%fused_computation.10.clone.1 | convolution fusion | flops 3222994944 | bytes 20316676 | tf_op jit(solution)/shard_map/while/body/eval_jaxpr/pvh,gh->pvg/dot_general | solution.py:48
  387.9 1.8 gather_fusion.1
  393.2 4.1 gather_fusion
  397.3 10.2 %fusion.45 = bf16[3,64,1024]{2,1,0:T(8,128)(2,1)} fusion(bf16[4,1024,8192]{2,1,0:T(8,128)(2,1)} %get-tuple-element.255, s32[]{:T(128)} %get-tuple-element.242, bf16[3,64,8192]{2,1,0:T(8,128)(2,1)S(1)} %gather_fusion, pred[3]{0:T(512)(128)(4,1)S(1)} %get-tuple-element.233), kind=kOutput, calls=%fused_computation.10.clone.1 | convolution fusion | flops 3222994944 | bytes 20316676 | tf_op jit(solution)/shard_map/while/body/eval_jaxpr/pvh,gh->pvg/dot_general | solution.py:48
  412.8 4.1 gather_fusion
  417.0 10.2 %fusion.45 = bf16[3,64,1024]{2,1,0:T(8,128)(2,1)} fusion(bf16[4,1024,8192]{2,1,0:T(8,128)(2,1)} %get-tuple-element.255, s32[]{:T(128)} %get-tuple-element.242, bf16[3,64,8192]{2,1,0:T(8,128)(2,1)S(1)} %gather_fusion, pred[3]{0:T(512)(128)(4,1)S(1)} %get-tuple-element.233), kind=kOutput, calls=%fused_computation.10.clone.1 | convolution fusion | flops 3222994944 | bytes 20316676 | tf_op jit(solution)/shard_map/while/body/eval_jaxpr/pvh,gh->pvg/dot_general | solution.py:48
  432.1 3.0 copy.14
  435.1 3.4 reshape.32
  438.6 12.8 %reduce-scatter.3.cloned.1.call-done = f32[1,64,256]{2,1,0:T(8,128)} async-done(((f32[2,64,256]{2,1,0:T(8,128)}), f32[1,64,256]{2,1,0:T(8,128)}) %reduce-scatter.3.cloned.1.call-update) | async-done | bytes 65552 | tf_op jit(solution)/shard_map/reduce_scatter | solution.py:62
  452.6 108.8 %all-reduce.3.cloned.1.call-done = f32[1,64,256]{2,1,0:T(8,128)} async-done(((f32[1,64,256]{2,1,0:T(8,128)}), f32[1,64,256]{2,1,0:T(8,128)}) %all-reduce.3.cloned.1.call-update) | async-done | bytes 65552
  (62 shorter events, 23.9 us)
Async XLA Ops:
  6.5 346.4 %all-gather.2.cloned.1.call-start = ((), (), s32[]{:S(2)}) async-start(), calls=%async_computation.1 | async-start | bytes 1572864 | tf_op jit(solution)/shard_map/all_gather | solution.py:11
  6.5 91.9 %copy-start = (bf16[2,4,4,8192]{3,2,1,0:T(4,128)(2,1)S(1)}, bf16[2,4,4,8192]{3,2,1,0:T(4,128)(2,1)}, u32[]{:S(2)}) copy-start(bf16[2,4,4,8192]{3,2,1,0:T(4,128)(2,1)} %param.7) | copy-start | bytes 1572868
  6.5 18.5 %collective-permute-start = (bf16[2,4,4,8192]{3,2,1,0:T(4,128)(2,1)}, bf16[2,4,4,8192]{3,2,1,0:T(4,128)(2,1)S(1)}, u32[]{:S(2)}, u32[]{:S(2)}) collective-permute-start(bf16[2,4,4,8192]{3,2,1,0:T(4,128)(2,1)} %param.7), channel_id=1, source_target_pairs={{0,30},{2,0},{4,2},{6,4},{8,6},{10,8},{12,10},{14,12},{16,14},{18,... | collective-permute-start | bytes 1572872 | tf_op jit(solution)/shard_map/ppermute | solution.py:24
  25.0 76.1 %copy-start.1 = (bf16[2,4,4,8192]{3,2,1,0:T(4,128)(2,1)}, bf16[2,4,4,8192]{3,2,1,0:T(4,128)(2,1)S(1)}, u32[]{:S(2)}) copy-start(bf16[2,4,4,8192]{3,2,1,0:T(4,128)(2,1)S(1)} %collective-permute-done) | copy-start | bytes 1572868
  26.7 24.1 %collective-permute-start.1 = (bf16[2,4,8,8192]{3,2,1,0:T(8,128)(2,1)S(1)}, bf16[2,4,8,8192]{3,2,1,0:T(8,128)(2,1)S(1)}, u32[]{:S(2)}, u32[]{:S(2)}) collective-permute-start(bf16[2,4,8,8192]{3,2,1,0:T(8,128)(2,1)S(1)} %pad_maximum_fusion.2), channel_id=1, source_target_pairs={{0,28},{2,30},{4,0},{6,2},{8,4},{10,6},{12,8},{14,10},{16,12},{18,... | collective-permute-start | bytes 3145736 | tf_op jit(solution)/shard_map/ppermute | solution.py:24
  52.7 48.5 %copy-start.2 = (s32[2,4]{1,0:T(2,128)S(1)}, s32[2,4]{1,0:T(2,128)}, u32[]{:S(2)}) copy-start(s32[2,4]{1,0:T(2,128)} %param.9) | copy-start | bytes 100
  52.7 45.7 %collective-permute-start.2 = (bf16[2,4,16,8192]{3,2,1,0:T(8,128)(2,1)S(1)}, bf16[2,4,16,8192]{3,2,1,0:T(8,128)(2,1)S(1)}, u32[]{:S(2)}, u32[]{:S(2)}) collective-permute-start(bf16[2,4,16,8192]{3,2,1,0:T(8,128)(2,1)S(1)} %pad_maximum_fusion.1), channel_id=1, source_target_pairs={{0,24},{2,26},{4,28},{6,30},{8,0},{10,2},{12,4},{14,6},{16,8},{18,... | collective-permute-start | bytes 6291464 | tf_op jit(solution)/shard_map/ppermute | solution.py:24
  101.1 180.5 %collective-permute-start.3 = (bf16[2,4,32,8192]{3,2,1,0:T(8,128)(2,1)}, bf16[2,4,32,8192]{3,2,1,0:T(8,128)(2,1)}, u32[]{:S(2)}, u32[]{:S(2)}) collective-permute-start(bf16[2,4,32,8192]{3,2,1,0:T(8,128)(2,1)} %pad_maximum_fusion), channel_id=1, source_target_pairs={{0,16},{2,18},{4,20},{6,22},{8,24},{10,26},{12,28},{14,30},{16,0},... | collective-permute-start | bytes 12582920 | tf_op jit(solution)/shard_map/ppermute | solution.py:24
  101.1 350.3 %reduce-scatter.3.cloned.1.call-start = ((), (), s32[]{:S(2)}) async-start(), calls=%async_computation.2 | async-start | bytes 196608 | tf_op jit(solution)/shard_map/reduce_scatter | solution.py:62
  431.5 19.9 %copy-start.3 = (u32[32]{0:T(128)S(1)}, u32[32]{0:T(128)}, u32[]{:S(2)}) copy-start(u32[32]{0:T(128)} %constant.110) | copy-start | bytes 388
  438.6 122.9 %all-reduce.3.cloned.1.call-start = ((), (), s32[]{:S(2)}) async-start(), calls=%async_computation.3 | async-start | bytes 131072
Sparse Core Ops, SparseCore 0:
  101.2 15.8 all-gather.1
  438.7 12.6 reduce-scatter.2
  456.9 104.5 all-reduce.2
